TPU v7x, 32 devices: a whole 2x2x4 slice. The times are simulated.
32 devices in a mesh: wide: 8 (over y, x, core), narrow: 4 (over z).
Axes of the slice: x: 2, y: 2, z: 4, core: 2. Of those that a mesh axis runs over, the one named last changes fastest.
Arguments:
- states: bfloat16 [16384, 1024], P(('wide', 'narrow')), may hold values from -6 to 6
- applied: bfloat16 [16384, 1024], P(('wide', 'narrow')), may hold values from -6 to 6
- rotation: bfloat16 [2, 1024, 256], P(None, 'wide', 'narrow'), may hold values from -0.1875 to 0.1875
- ritz: float32 [2, 256], replicated, may hold values from 0.5 to 4
- potential: float32 [16384], P(('wide', 'narrow')), may hold values from 0.5 to 8
Outputs:
- rotated: bfloat16 [16384, 2, 256], P(('wide', 'narrow'))
- correction: bfloat16 [16384, 2, 256], P(('wide', 'narrow'))
- margin: float32 [2, 1024, 256], P(None, 'wide', 'narrow')
All inputs are finite; a program needn't handle non-finite values.
Results may differ from a plain program's by a relative error of at most 0.0095.
Values may be sent and summed in bfloat16 or wider, within the bound.
A program may use at most 64 MiB of HBM per device.

v0:
```python
import math
import jax
import jax.numpy as jnp
from jax import lax
from jax.sharding import PartitionSpec as P


def per_device(states, applied, rotation, ritz, potential):
    row_count = states.shape[0]
    total_rows = row_count * lax.axis_size("wide") * lax.axis_size("narrow")
    factor = 1.0 / math.sqrt(total_rows)
    contract = (((0,), (0,)), ((), ()))
    rotated_list = []
    correction_list = []
    margin_list = []
    for window in range(rotation.shape[0]):
        q_local = rotation[window]
        q_tall = lax.all_gather(q_local, "wide", axis=0, tiled=True)
        q_full = lax.all_gather(q_tall, "narrow", axis=1, tiled=True)
        plain = jnp.dot(states, q_full, preferred_element_type=jnp.float32)
        mapped = jnp.dot(applied, q_full, preferred_element_type=jnp.float32)
        eigen_values = ritz[window]
        residual = mapped - plain * eigen_values[None, :]
        fixed = (residual / (potential[:, None] + eigen_values[None, :])).astype(jnp.bfloat16)
        partial_value = lax.psum_scatter(
            lax.dot_general(states, fixed, contract, preferred_element_type=jnp.float32).astype(
                jnp.bfloat16
            ),
            "wide",
            scatter_dimension=0,
            tiled=True,
        )
        summed = lax.psum_scatter(partial_value, "narrow", scatter_dimension=1, tiled=True).astype(
            jnp.float32
        )
        rotated_list.append(plain.astype(jnp.bfloat16))
        correction_list.append(fixed)
        margin_list.append(summed * factor)
    return (
        jnp.stack(rotated_list, axis=1),
        jnp.stack(correction_list, axis=1),
        jnp.stack(margin_list, axis=0),
    )


def solution(mesh):
    placed = (
        P(("wide", "narrow"), None),
        P(("wide", "narrow"), None),
        P(None, "wide", "narrow"),
        P(),
        P(("wide", "narrow")),
    )
    return jax.shard_map(
        per_device,
        mesh=mesh,
        in_specs=placed,
        out_specs=(
            P(("wide", "narrow"), None, None),
            P(("wide", "narrow"), None, None),
            P(None, "wide", "narrow"),
        ),
        check_vma=False,
    )
```

profile of v0, /device:TPU:0, one launch (start us, length us, event | category | flops | bytes accessed | tf_op | source)
XLA Modules:
  0.0 160.5 jit_solution(8119105058409660867)
XLA Ops:
  7.2 0.8 fusion.13
  8.0 0.7 fusion.12
  8.7 10.5 %all-gather.2 = bf16[1,1024,64]{1,2,0:T(8,128)(2,1)S(1)} all-gather(bf16[1,128,64]{1,2,0:T(8,128)(2,1)S(1)} %get-tuple-element.10), channel_id=4, replica_groups=mesh['wide'=8,'narrow'=4] {'wide'}, dimensions={1}, use_global_device_ids=true | all-gather | bytes 147456 | tf_op jit(solution)/shard_map/all_gather | solution.py:18
  19.3 16.3 %all-gather.3 = bf16[1,1024,256]{1,2,0:T(8,128)(2,1)S(1)} all-gather(bf16[1,1024,64]{1,2,0:T(8,128)(2,1)S(1)} %all-gather.2), channel_id=5, replica_groups=mesh['wide'=8,'narrow'=4] {'narrow'}, dimensions={2}, use_global_device_ids=true | all-gather | bytes 655360 | tf_op jit(solution)/shard_map/all_gather | solution.py:19
  35.6 0.5 fusion.7
  36.1 0.7 copy-done.1
  36.8 0.5 fusion.4
  37.8 1.0 copy.14
  38.9 9.0 %all-gather = bf16[1,1024,64]{1,2,0:T(8,128)(2,1)S(1)} all-gather(bf16[1,128,64]{1,2,0:T(8,128)(2,1)S(1)} %get-tuple-element.9), channel_id=2, replica_groups=mesh['wide'=8,'narrow'=4] {'wide'}, dimensions={1}, use_global_device_ids=true | all-gather | bytes 147456 | tf_op jit(solution)/shard_map/all_gather | solution.py:18
  47.9 16.6 %all-gather.1 = bf16[1,1024,256]{1,2,0:T(8,128)(2,1)S(1)} all-gather(bf16[1,1024,64]{1,2,0:T(8,128)(2,1)S(1)} %all-gather), channel_id=3, replica_groups=mesh['wide'=8,'narrow'=4] {'narrow'}, dimensions={2}, use_global_device_ids=true | all-gather | bytes 655360 | tf_op jit(solution)/shard_map/all_gather | solution.py:19
  65.0 0.7 copy-done.2
  65.7 0.5 fusion.5
  66.6 1.0 copy.12
  67.8 5.8 %reduce-scatter.15.cloned.1.call-done = bf16[128,256]{1,0:T(8,128)(2,1)} async-done(((bf16[1024,256]{1,0:T(8,128)(2,1)}), bf16[128,256]{1,0:T(8,128)(2,1)}) %reduce-scatter.15.cloned.1.call-update) | async-done | bytes 65552
  73.6 1.6 copy.15
  75.3 1.3 copy.10
  76.7 1.3 copy.11
  78.0 32.8 %reduce-scatter.13.cloned.1.call-done = bf16[128,256]{1,0:T(8,128)(2,1)} async-done(((bf16[1024,256]{1,0:T(8,128)(2,1)}), bf16[128,256]{1,0:T(8,128)(2,1)}) %reduce-scatter.13.cloned.1.call-update) | async-done | bytes 65552
  110.9 1.6 copy.13
  112.5 20.6 %reduce-scatter.11.cloned.1.call-done = bf16[128,64]{0,1:T(8,128)(2,1)} async-done(((bf16[128,256]{0,1:T(8,128)(2,1)}), bf16[128,64]{0,1:T(8,128)(2,1)}) %reduce-scatter.11.cloned.1.call-update) | async-done | bytes 16400 | tf_op jit(solution)/shard_map/reduce_scatter | solution.py:33
  133.0 0.7 multiply_bitcast_fusion
  133.7 18.9 %reduce-scatter.9.cloned.1.call-done = bf16[128,64]{0,1:T(8,128)(2,1)} async-done(((bf16[128,256]{0,1:T(8,128)(2,1)}), bf16[128,64]{0,1:T(8,128)(2,1)}) %reduce-scatter.9.cloned.1.call-update) | async-done | bytes 16400 | tf_op jit(solution)/shard_map/reduce_scatter | solution.py:33
  152.6 0.7 multiply_bitcast_fusion.1
  153.3 0.6 pad_maximum_fusion.2
  (21 shorter events, 1.8 us)
Async XLA Ops:
  7.2 28.4 %copy-start = (bf16[512,1024]{1,0:T(8,128)(2,1)S(1)}, bf16[512,1024]{1,0:T(8,128)(2,1)}, u32[]{:S(2)}) copy-start(bf16[512,1024]{1,0:T(8,128)(2,1)} %param.5) | copy-start | bytes 3145732
  7.2 66.4 %reduce-scatter.15.cloned.1.call-start = ((), (), s32[]{:S(2)}) async-start(), calls=%async_computation.7 | async-start | bytes 589824
  35.6 1.2 copy-start.1
  36.1 0.7 copy-start.3
  38.8 72.1 %reduce-scatter.13.cloned.1.call-start = ((), (), s32[]{:S(2)}) async-start(), calls=%async_computation.6 | async-start | bytes 589824
  64.5 1.2 copy-start.2
  67.7 65.3 %reduce-scatter.11.cloned.1.call-start = ((), (), s32[]{:S(2)}) async-start(), calls=%async_computation.5 | async-start | bytes 81920 | tf_op jit(solution)/shard_map/reduce_scatter | solution.py:33
  75.2 77.4 %reduce-scatter.9.cloned.1.call-start = ((), (), s32[]{:S(2)}) async-start(), calls=%async_computation.4 | async-start | bytes 81920 | tf_op jit(solution)/shard_map/reduce_scatter | solution.py:33
Sparse Core Ops, SparseCore 0:
  38.9 34.6 reduce-scatter.14
  76.7 34.1 reduce-scatter.12
  113.7 19.2 reduce-scatter.10
  135.1 17.4 reduce-scatter.8
where the time goes:
time: 161 us; the launch traced here: 160 us
  waiting for transfers between devices  78.1 us (49%)
  blocking collectives  52.5 us (33%)
  between operations  13.9 us (9%)
  local copies, waits for them, and re-layouts  10.8 us (7%)
  matrix products  2.82 us (2%)
  other arithmetic  2.24 us (1%)
    reduce_scatter x2, waiting for transfers between devices, per_device(): lax.psum_scatter(partial_value, 'narrow', scatter_dimension=1, tiled=True)  39.4 us
    unnamed x6, waiting for transfers between devices  38.7 us
    all_gather x2, blocking collectives, per_device(): q_full = lax.all_gather(q_tall, 'narrow', axis=1, tiled=True)  32.9 us
    all_gather x2, blocking collectives, per_device(): q_tall = lax.all_gather(q_local, 'wide', axis=0, tiled=True)  19.6 us
    unnamed x14, local copies, waits for them, and re-layouts  9.3 us
  transfers between devices with their start and end apart: 4, of which 4 were waited for; matrix products, arithmetic and copies ran while one was open for 6% of the time, Pallas kernels for 0%

commit v1 on v0

--- a/solution.py
+++ b/solution.py
@@ -3,6 +3,19 @@
 import jax.numpy as jnp
 from jax import lax
 from jax.sharding import PartitionSpec as P
+
+
+def terms_finish(sample, which_axis="wide"):
+    n_dev_all = lax.axis_size(which_axis)
+    pool = [(i, (i + 1) % n_dev_all) for i in range(n_dev_all)]
+
+    def run_shelves(spare):
+        if len(spare) == n_dev_all:
+            return spare
+        return run_shelves([lax.ppermute(spare[0], which_axis, perm=pool), *spare])
+
+    tmp = jnp.concatenate(run_shelves([sample]), axis=0)
+    return jnp.roll(tmp, shift=(lax.axis_index(which_axis) + 1) * sample.shape[0], axis=0)
 
 
 def per_device(states, applied, rotation, ritz, potential):
@@ -15,7 +28,7 @@
     margin_list = []
     for window in range(rotation.shape[0]):
         q_local = rotation[window]
-        q_tall = lax.all_gather(q_local, "wide", axis=0, tiled=True)
+        q_tall = terms_finish(q_local)
         q_full = lax.all_gather(q_tall, "narrow", axis=1, tiled=True)
         plain = jnp.dot(states, q_full, preferred_element_type=jnp.float32)
         mapped = jnp.dot(applied, q_full, preferred_element_type=jnp.float32)

time: 161 us -> 195 us (1.21)
  waiting for transfers between devices: 78.1 us -> 125 us
  blocking collectives: 52.5 us -> 33.2 us
  starting transfers between devices: 0.16 us -> 4.96 us
    ppermute x0 -> x14, waiting for transfers between devices: none -> 24.4 us  [run_shelves(): return run_shelves([lax.ppermute(spare[0], which_axis, perm=pool), *spare])]
    unnamed x6, waiting for transfers between devices: 38.7 us -> 61.6 us
    all_gather x2 -> x0, blocking collectives: 19.6 us -> none  [per_device(): q_tall = lax.all_gather(q_local, 'wide', axis=0, tiled=True)]
    ppermute x0 -> x14, starting transfers between devices: none -> 4.79 us  [run_shelves(): return run_shelves([lax.ppermute(spare[0], which_axis, perm=pool), *spare])]
    unnamed x14 -> x36, local copies, waits for them, and re-layouts: 9.3 us -> 10.4 us
  transfers between devices with their start and end apart: 4 -> 18, of which waited for: 4 -> 18; matrix products, arithmetic and copies ran while one was open for 6% -> 4% of each run, Pallas kernels for 0% -> 0%
where the time goes in v1:
time: 195 us; the launch traced here: 194 us
  waiting for transfers between devices  125 us (64%)
  blocking collectives  33.2 us (17%)
  between operations  14 us (7%)
  local copies, waits for them, and re-layouts  11.2 us (6%)
  starting transfers between devices  4.96 us (3%)
  matrix products  2.77 us (1%)
  other arithmetic  2.43 us (1%)
    unnamed x6, waiting for transfers between devices  61.6 us
    reduce_scatter x2, waiting for transfers between devices, per_device(): lax.psum_scatter(partial_value, 'narrow', scatter_dimension=1, tiled=True)  39.4 us
    all_gather x2, blocking collectives, per_device(): q_full = lax.all_gather(q_tall, 'narrow', axis=1, tiled=True)  33.2 us
    ppermute x14, waiting for transfers between devices, run_shelves(): return run_shelves([lax.ppermute(spare[0], which_axis, perm=pool), *spare])  24.4 us
    unnamed x36, local copies, waits for them, and re-layouts  10.4 us
    ppermute x14, starting transfers between devices, run_shelves(): return run_shelves([lax.ppermute(spare[0], which_axis, perm=pool), *spare])  4.79 us
  transfers between devices with their start and end apart: 18, of which 18 were waited for; matrix products, arithmetic and copies ran while one was open for 4% of the time, Pallas kernels for 0%

profile of v1, /device:TPU:0, one launch (start us, length us, event | category | flops | bytes accessed | tf_op | source)
XLA Modules:
  0.0 194.1 jit_solution(587853179236058857)
XLA Ops:
  7.2 0.8 slice_bitcast_fusion.1
  8.5 2.6 %collective-permute-start = (bf16[128,64]{0,1:T(8,128)(2,1)S(1)}, bf16[128,64]{0,1:T(8,128)(2,1)S(1)}, u32[]{:S(2)}, u32[]{:S(2)}) collective-permute-start(bf16[128,64]{0,1:T(8,128)(2,1)S(1)} %get-tuple-element.12), channel_id=1, source_target_pairs={{0,4},{4,8},{8,12},{12,16},{16,20},{20,24},{24,28},{28,0},{1,5},{5... | collective-permute-start | bytes 49160 | tf_op jit(solution)/shard_map/ppermute | solution.py:15
  11.1 1.7 collective-permute-done.7
  13.0 1.3 collective-permute-start.1
  14.3 2.6 %collective-permute-done.8 = bf16[128,64]{0,1:T(8,128)(2,1)S(1)} collective-permute-done((bf16[128,64]{0,1:T(8,128)(2,1)S(1)}, bf16[128,64]{0,1:T(8,128)(2,1)S(1)}, u32[]{:S(2)}, u32[]{:S(2)}) %collective-permute-start.8) | collective-permute-done | bytes 16416 | tf_op jit(solution)/shard_map/ppermute | solution.py:15
  17.5 3.5 %collective-permute-done.9 = bf16[128,64]{0,1:T(8,128)(2,1)S(1)} collective-permute-done((bf16[128,64]{0,1:T(8,128)(2,1)S(1)}, bf16[128,64]{0,1:T(8,128)(2,1)S(1)}, u32[]{:S(2)}, u32[]{:S(2)}) %collective-permute-start.9) | collective-permute-done | bytes 16416 | tf_op jit(solution)/shard_map/ppermute | solution.py:15
  21.1 3.9 %collective-permute-done.10 = bf16[128,64]{0,1:T(8,128)(2,1)S(1)} collective-permute-done((bf16[128,64]{0,1:T(8,128)(2,1)S(1)}, bf16[128,64]{0,1:T(8,128)(2,1)S(1)}, u32[]{:S(2)}, u32[]{:S(2)}) %collective-permute-start.10) | collective-permute-done | bytes 16416 | tf_op jit(solution)/shard_map/ppermute | solution.py:15
  25.2 3.9 %collective-permute-done.11 = bf16[128,64]{0,1:T(8,128)(2,1)S(1)} collective-permute-done((bf16[128,64]{0,1:T(8,128)(2,1)S(1)}, bf16[128,64]{0,1:T(8,128)(2,1)S(1)}, u32[]{:S(2)}, u32[]{:S(2)}) %collective-permute-start.11) | collective-permute-done | bytes 16416 | tf_op jit(solution)/shard_map/ppermute | solution.py:15
  29.3 3.9 %collective-permute-done.12 = bf16[128,64]{0,1:T(8,128)(2,1)S(1)} collective-permute-done((bf16[128,64]{0,1:T(8,128)(2,1)S(1)}, bf16[128,64]{0,1:T(8,128)(2,1)S(1)}, u32[]{:S(2)}, u32[]{:S(2)}) %collective-permute-start.12) | collective-permute-done | bytes 16416 | tf_op jit(solution)/shard_map/ppermute | solution.py:15
  33.3 3.9 %collective-permute-done.13 = bf16[128,64]{0,1:T(8,128)(2,1)S(1)} collective-permute-done((bf16[128,64]{0,1:T(8,128)(2,1)S(1)}, bf16[128,64]{0,1:T(8,128)(2,1)S(1)}, u32[]{:S(2)}, u32[]{:S(2)}) %collective-permute-start.13) | collective-permute-done | bytes 16416 | tf_op jit(solution)/shard_map/ppermute | solution.py:15
  38.4 17.2 %all_gather.7 = bf16[1024,256]{0,1:T(8,128)(2,1)S(1)} all-gather(bf16[1024,64]{0,1:T(8,128)(2,1)S(1)} %fusion.8), channel_id=1, replica_groups=mesh['wide'=8,'narrow'=4] {'narrow'}, dimensions={1}, use_global_device_ids=true | all-gather | bytes 655360 | tf_op jit(solution)/shard_map/all_gather | solution.py:32
  55.6 16.1 %all_gather.6 = bf16[1024,256]{0,1:T(8,128)(2,1)S(1)} all-gather(bf16[1024,64]{0,1:T(8,128)(2,1)S(1)} %fusion.9), channel_id=1, replica_groups=mesh['wide'=8,'narrow'=4] {'narrow'}, dimensions={1}, use_global_device_ids=true | all-gather | bytes 655360 | tf_op jit(solution)/shard_map/all_gather | solution.py:32
  72.2 0.7 copy-done.5
  73.8 1.0 copy.14
  75.4 0.7 copy-done.6
  77.7 1.0 copy.12
  78.9 28.3 %reduce-scatter.15.cloned.1.call-done = bf16[128,256]{1,0:T(8,128)(2,1)} async-done(((bf16[1024,256]{1,0:T(8,128)(2,1)}), bf16[128,256]{1,0:T(8,128)(2,1)}) %reduce-scatter.15.cloned.1.call-update) | async-done | bytes 65552
  107.2 1.6 copy.15
  108.9 1.1 copy.10
  110.1 1.1 copy.11
  111.2 33.3 %reduce-scatter.13.cloned.1.call-done = bf16[128,256]{1,0:T(8,128)(2,1)} async-done(((bf16[1024,256]{1,0:T(8,128)(2,1)}), bf16[128,256]{1,0:T(8,128)(2,1)}) %reduce-scatter.13.cloned.1.call-update) | async-done | bytes 65552
  144.4 1.6 copy.13
  146.0 20.6 %reduce-scatter.11.cloned.1.call-done = bf16[128,64]{0,1:T(8,128)(2,1)} async-done(((bf16[128,256]{0,1:T(8,128)(2,1)}), bf16[128,64]{0,1:T(8,128)(2,1)}) %reduce-scatter.11.cloned.1.call-update) | async-done | bytes 16400 | tf_op jit(solution)/shard_map/reduce_scatter | solution.py:46
  167.3 18.9 %reduce-scatter.9.cloned.1.call-done = bf16[128,64]{0,1:T(8,128)(2,1)} async-done(((bf16[128,256]{0,1:T(8,128)(2,1)}), bf16[128,64]{0,1:T(8,128)(2,1)}) %reduce-scatter.9.cloned.1.call-update) | async-done | bytes 16400 | tf_op jit(solution)/shard_map/reduce_scatter | solution.py:46
  (72 shorter events, 9.0 us)
Async XLA Ops:
  7.2 64.5 %copy-start = (bf16[512,1024]{1,0:T(8,128)(2,1)S(1)}, bf16[512,1024]{1,0:T(8,128)(2,1)}, u32[]{:S(2)}) copy-start(bf16[512,1024]{1,0:T(8,128)(2,1)} %param.7) | copy-start | bytes 3145732
  7.2 100.0 %reduce-scatter.15.cloned.1.call-start = ((), (), s32[]{:S(2)}) async-start(), calls=%async_computation.7 | async-start | bytes 589824
  8.0 25.1 %copy-start.4 = (f32[2,256]{1,0:T(2,128)S(1)}, f32[2,256]{1,0:T(2,128)}, u32[]{:S(2)}) copy-start(f32[2,256]{1,0:T(2,128)} %param.10) | copy-start | bytes 6148
  8.0 4.8 %collective-permute-start.7 = (bf16[128,64]{0,1:T(8,128)(2,1)S(1)}, bf16[128,64]{0,1:T(8,128)(2,1)S(1)}, u32[]{:S(2)}, u32[]{:S(2)}) collective-permute-start(bf16[128,64]{0,1:T(8,128)(2,1)S(1)} %get-tuple-element.13), channel_id=1, source_target_pairs={{0,4},{4,8},{8,12},{12,16},{16,20},{20,24},{24,28},{28,0},{1,5},{5... | collective-permute-start | bytes 49160 | tf_op jit(solution)/shard_map/ppermute | solution.py:15
  8.5 4.5 %collective-permute-start = (bf16[128,64]{0,1:T(8,128)(2,1)S(1)}, bf16[128,64]{0,1:T(8,128)(2,1)S(1)}, u32[]{:S(2)}, u32[]{:S(2)}) collective-permute-start(bf16[128,64]{0,1:T(8,128)(2,1)S(1)} %get-tuple-element.12), channel_id=1, source_target_pairs={{0,4},{4,8},{8,12},{12,16},{16,20},{20,24},{24,28},{28,0},{1,5},{5... | collective-permute-start | bytes 49160 | tf_op jit(solution)/shard_map/ppermute | solution.py:15
  12.8 4.1 %collective-permute-start.8 = (bf16[128,64]{0,1:T(8,128)(2,1)S(1)}, bf16[128,64]{0,1:T(8,128)(2,1)S(1)}, u32[]{:S(2)}, u32[]{:S(2)}) collective-permute-start(bf16[128,64]{0,1:T(8,128)(2,1)S(1)} %collective-permute-done.7), channel_id=1, source_target_pairs={{0,4},{4,8},{8,12},{12,16},{16,20},{20,24},{24,28},{28,0},{1,5},{5... | collective-permute-start | bytes 49160 | tf_op jit(solution)/shard_map/ppermute | solution.py:15
  13.0 4.1 %collective-permute-start.1 = (bf16[128,64]{0,1:T(8,128)(2,1)S(1)}, bf16[128,64]{0,1:T(8,128)(2,1)S(1)}, u32[]{:S(2)}, u32[]{:S(2)}) collective-permute-start(bf16[128,64]{0,1:T(8,128)(2,1)S(1)} %collective-permute-done), channel_id=1, source_target_pairs={{0,4},{4,8},{8,12},{12,16},{16,20},{20,24},{24,28},{28,0},{1,5},{5... | collective-permute-start | bytes 49160 | tf_op jit(solution)/shard_map/ppermute | solution.py:15
  16.9 4.1 %collective-permute-start.9 = (bf16[128,64]{0,1:T(8,128)(2,1)S(1)}, bf16[128,64]{0,1:T(8,128)(2,1)S(1)}, u32[]{:S(2)}, u32[]{:S(2)}) collective-permute-start(bf16[128,64]{0,1:T(8,128)(2,1)S(1)} %collective-permute-done.8), channel_id=1, source_target_pairs={{0,4},{4,8},{8,12},{12,16},{16,20},{20,24},{24,28},{28,0},{1,5},{5... | collective-permute-start | bytes 49160 | tf_op jit(solution)/shard_map/ppermute | solution.py:15
  17.1 4.1 %collective-permute-start.2 = (bf16[128,64]{0,1:T(8,128)(2,1)S(1)}, bf16[128,64]{0,1:T(8,128)(2,1)S(1)}, u32[]{:S(2)}, u32[]{:S(2)}) collective-permute-start(bf16[128,64]{0,1:T(8,128)(2,1)S(1)} %collective-permute-done.1), channel_id=1, source_target_pairs={{0,4},{4,8},{8,12},{12,16},{16,20},{20,24},{24,28},{28,0},{1,5},{5... | collective-permute-start | bytes 49160 | tf_op jit(solution)/shard_map/ppermute | solution.py:15
  21.0 4.1 %collective-permute-start.10 = (bf16[128,64]{0,1:T(8,128)(2,1)S(1)}, bf16[128,64]{0,1:T(8,128)(2,1)S(1)}, u32[]{:S(2)}, u32[]{:S(2)}) collective-permute-start(bf16[128,64]{0,1:T(8,128)(2,1)S(1)} %collective-permute-done.9), channel_id=1, source_target_pairs={{0,4},{4,8},{8,12},{12,16},{16,20},{20,24},{24,28},{28,0},{1,5},{5... | collective-permute-start | bytes 49160 | tf_op jit(solution)/shard_map/ppermute | solution.py:15
  21.1 4.1 %collective-permute-start.3 = (bf16[128,64]{0,1:T(8,128)(2,1)S(1)}, bf16[128,64]{0,1:T(8,128)(2,1)S(1)}, u32[]{:S(2)}, u32[]{:S(2)}) collective-permute-start(bf16[128,64]{0,1:T(8,128)(2,1)S(1)} %collective-permute-done.2), channel_id=1, source_target_pairs={{0,4},{4,8},{8,12},{12,16},{16,20},{20,24},{24,28},{28,0},{1,5},{5... | collective-permute-start | bytes 49160 | tf_op jit(solution)/shard_map/ppermute | solution.py:15
  25.0 4.1 %collective-permute-start.11 = (bf16[128,64]{0,1:T(8,128)(2,1)S(1)}, bf16[128,64]{0,1:T(8,128)(2,1)S(1)}, u32[]{:S(2)}, u32[]{:S(2)}) collective-permute-start(bf16[128,64]{0,1:T(8,128)(2,1)S(1)} %collective-permute-done.10), channel_id=1, source_target_pairs={{0,4},{4,8},{8,12},{12,16},{16,20},{20,24},{24,28},{28,0},{1,5},{5... | collective-permute-start | bytes 49160 | tf_op jit(solution)/shard_map/ppermute | solution.py:15
  25.2 4.1 %collective-permute-start.4 = (bf16[128,64]{0,1:T(8,128)(2,1)S(1)}, bf16[128,64]{0,1:T(8,128)(2,1)S(1)}, u32[]{:S(2)}, u32[]{:S(2)}) collective-permute-start(bf16[128,64]{0,1:T(8,128)(2,1)S(1)} %collective-permute-done.3), channel_id=1, source_target_pairs={{0,4},{4,8},{8,12},{12,16},{16,20},{20,24},{24,28},{28,0},{1,5},{5... | collective-permute-start | bytes 49160 | tf_op jit(solution)/shard_map/ppermute | solution.py:15
  29.1 4.1 %collective-permute-start.12 = (bf16[128,64]{0,1:T(8,128)(2,1)S(1)}, bf16[128,64]{0,1:T(8,128)(2,1)S(1)}, u32[]{:S(2)}, u32[]{:S(2)}) collective-permute-start(bf16[128,64]{0,1:T(8,128)(2,1)S(1)} %collective-permute-done.11), channel_id=1, source_target_pairs={{0,4},{4,8},{8,12},{12,16},{16,20},{20,24},{24,28},{28,0},{1,5},{5... | collective-permute-start | bytes 49160 | tf_op jit(solution)/shard_map/ppermute | solution.py:15
  29.3 4.1 %collective-permute-start.5 = (bf16[128,64]{0,1:T(8,128)(2,1)S(1)}, bf16[128,64]{0,1:T(8,128)(2,1)S(1)}, u32[]{:S(2)}, u32[]{:S(2)}) collective-permute-start(bf16[128,64]{0,1:T(8,128)(2,1)S(1)} %collective-permute-done.4), channel_id=1, source_target_pairs={{0,4},{4,8},{8,12},{12,16},{16,20},{20,24},{24,28},{28,0},{1,5},{5... | collective-permute-start | bytes 49160 | tf_op jit(solution)/shard_map/ppermute | solution.py:15
  33.1 4.1 %collective-permute-start.13 = (bf16[128,64]{0,1:T(8,128)(2,1)S(1)}, bf16[128,64]{0,1:T(8,128)(2,1)S(1)}, u32[]{:S(2)}, u32[]{:S(2)}) collective-permute-start(bf16[128,64]{0,1:T(8,128)(2,1)S(1)} %collective-permute-done.12), channel_id=1, source_target_pairs={{0,4},{4,8},{8,12},{12,16},{16,20},{20,24},{24,28},{28,0},{1,5},{5... | collective-permute-start | bytes 49160 | tf_op jit(solution)/shard_map/ppermute | solution.py:15
  33.3 4.1 %collective-permute-start.6 = (bf16[128,64]{0,1:T(8,128)(2,1)S(1)}, bf16[128,64]{0,1:T(8,128)(2,1)S(1)}, u32[]{:S(2)}, u32[]{:S(2)}) collective-permute-start(bf16[128,64]{0,1:T(8,128)(2,1)S(1)} %collective-permute-done.5), channel_id=1, source_target_pairs={{0,4},{4,8},{8,12},{12,16},{16,20},{20,24},{24,28},{28,0},{1,5},{5... | collective-permute-start | bytes 49160 | tf_op jit(solution)/shard_map/ppermute | solution.py:15
  37.4 0.8 copy-start.3
  71.7 1.2 copy-start.5
  74.8 69.6 %reduce-scatter.13.cloned.1.call-start = ((), (), s32[]{:S(2)}) async-start(), calls=%async_computation.6 | async-start | bytes 589824
  74.9 1.2 copy-start.6
  78.8 87.8 %reduce-scatter.11.cloned.1.call-start = ((), (), s32[]{:S(2)}) async-start(), calls=%async_computation.5 | async-start | bytes 81920 | tf_op jit(solution)/shard_map/reduce_scatter | solution.py:46
  108.8 77.4 %reduce-scatter.9.cloned.1.call-start = ((), (), s32[]{:S(2)}) async-start(), calls=%async_computation.4 | async-start | bytes 81920 | tf_op jit(solution)/shard_map/reduce_scatter | solution.py:46
  108.9 1.1 copy-start.2
  (2 other events, 1.4 us)
Sparse Core Ops, SparseCore 0:
  75.0 32.1 reduce-scatter.14
  110.3 34.1 reduce-scatter.12
  147.3 19.2 reduce-scatter.10
  168.7 17.4 reduce-scatter.8
